TPU v7x, 128 devices: a whole 4x4x4 slice. The times are simulated.
128 devices in a mesh: grain: 32 (over y, z, core), cell: 4 (over x).
Axes of the slice: x: 4, y: 4, z: 4, core: 2. Of those that a mesh axis runs over, the one named last changes fastest.
Arguments:
- displacement: float32 [4096, 3, 768], P(('grain', 'cell')), may hold values from -0.1 to 0.1
- velocity: float32 [4096, 3, 768], P(('grain', 'cell')), may hold values from -6 to 6
- centers: float32 [3, 4096], P(None, ('grain', 'cell')), may hold values from -4 to 4
- tile_list: int32 [4096, 4, 2], P(('grain', 'cell')), may hold values from 0 to 5
- broken_bits: int32 [4096, 4, 2048], P(('grain', 'cell')), may hold values from 0 to 255, as said below
- surface_nodes: int32 [4096, 512], P(('grain', 'cell')), may hold values from 0 to 767, as said below
- send_order: int32 [128, 128], P(('grain', 'cell')), may hold values from 0 to 127, each once within a row
- pair_list: int32 [128, 128, 2], P(('grain', 'cell')), may hold values from 0 to 127
- pair_count: int32 [128], P(('grain', 'cell')), may hold values from 1 to 128, 8192 in all
Outputs:
- force: float32 [4096, 3, 768], P(('grain', 'cell'))
- new_velocity: float32 [4096, 3, 768], P(('grain', 'cell'))
Inputs may be any that keep to these rules, and one draw needn't show every extreme that they name: `surface_nodes`: within a grain the 512 surface node indices are distinct. `send_order`: each row is a permutation of the device's 128 surface blocks; position p goes to device p div 1, so every device receives exactly 1 block from each device. `broken_bits`: each word packs 8 broken flags, any bit pattern.
All inputs are finite; a program needn't handle non-finite values. No bound on the sum of `pair_count` on one device may be relied on, other than what follows from the above.
Results may differ from a plain program's by a relative error of at most 0.0003.
Values sent between devices are 32-bit elements; how exact they have to be, the bound alone decides.
No kernel may reach another device: no remote copies, remote signals or barrier semaphores. Data moves between devices by JAX's collectives and lax.ppermute only.
A program may use at most 64 MiB of HBM per device.

v0:
```python
import functools
import math

import jax
import jax.numpy as jnp
from jax import lax
from jax.experimental import pallas as pl
from jax.experimental.pallas import tpu as pltpu
from jax.sharding import PartitionSpec as P

BLK = 128
SB = 4
GRAINS_DEV = 32
NODES = 768
NB = NODES // BLK
SLOTS = 128
GROUPS = GRAINS_DEV // 8

CONTACT_STIFF = 0.02
CONTACT_DAMP = 0.05
CONTACT_RANGE = 9.0
TIME_STEP = 0.5
BOND_STIFF = 5.0
HORIZON = 3.0
ORIGIN = (3.5, 3.5, 5.5)
LANE = 1
F32 = jnp.float32
BF16 = jnp.bfloat16
MIB = 1 << 20
REACH = 2
ACROSS = (((1,), (1,)), ((), ()))
DOWN = (((1,), (0,)), ((), ()))


def pieces(value, count):
    parts = []
    rest = value
    for step in range(count):
        head = rest.astype(BF16).astype(F32)
        parts.append(head)
        if step + 1 < count:
            rest = rest - head
    return parts


def halves(value):
    high = value.astype(BF16)
    return high, (value - high.astype(F32)).astype(BF16)


def lane_gather(source, index):
    return jnp.take_along_axis(source, index, axis=1, mode="promise_in_bounds")


def lane_iota(shape):
    return lax.broadcasted_iota(jnp.int32, shape, len(shape) - 1)


def sublane_iota(shape):
    return lax.broadcasted_iota(jnp.int32, shape, 0)


def gather_kernel(send_ref, disp_ref, vel_ref, centers_ref, nodes_ref, out_ref, state_ref):
    for group in range(GROUPS):
        grains = pl.ds(8 * group, 8)
        own = lane_iota((8, GRAINS_DEV)) == sublane_iota((8, GRAINS_DEV)) + 8 * group
        offsets = [
            jnp.sum(
                jnp.where(own, jnp.broadcast_to(centers_ref[c : c + 1, :], own.shape), 0.0),
                axis=1,
                keepdims=True,
            )
            for c in range(3)
        ]
        for k in range(SB):
            node = nodes_ref[grains, k * BLK : (k + 1) * BLK]
            lane = node & (BLK - 1)
            block = node >> 7
            rest = (node & 7, (node >> 3) & 7, node >> 6)
            for c in range(6):
                ref = disp_ref if c < 3 else vel_ref
                value = lane_gather(ref[c % 3, grains, :BLK], lane)
                for a in range(1, NB):
                    source = ref[c % 3, grains, a * BLK : (a + 1) * BLK]
                    value = jnp.where(block == a, lane_gather(source, lane), value)
                if c < 3:
                    value = rest[c].astype(F32) + value + offsets[c]
                state_ref[pl.ds((group * SB + k) * 48 + c * 8, 8), :] = value
    for d in range(SLOTS):
        block = send_ref[0, d]
        grain = block >> 2
        row = ((grain >> 3) * SB + (block & 3)) * 48 + (grain & 7)
        out_ref[6 * d : 6 * d + 6, :] = state_ref[pl.ds(row, 6, stride=8), :]


def surface_blocks(send_order, displacement, velocity, centers, surface_nodes):
    vmem = pl.BlockSpec(memory_space=pltpu.VMEM)
    return pl.pallas_call(
        gather_kernel,
        out_shape=jax.ShapeDtypeStruct((SLOTS * 6, BLK), F32),
        in_specs=[pl.BlockSpec(memory_space=pltpu.SMEM), vmem, vmem, vmem, vmem],
        out_specs=vmem,
        scratch_shapes=[pltpu.VMEM((SLOTS * 6, BLK), F32)],
        compiler_params=pltpu.CompilerParams(vmem_limit_bytes=8 * MIB),
        name="surface_blocks",
    )(send_order, displacement, velocity, centers, surface_nodes)


PAIR_UNROLL = 16


def contact_kernel(count_ref, pairs_ref, state_ref, out_ref, left_ref, right_ref, slide_ref, acc_ref):
    scale = math.log2(math.e) / CONTACT_RANGE
    one = jnp.ones((8, BLK), F32)
    pad = jnp.zeros((8, BLK), F32)

    def put(ref, rows, group, values):
        for n, value in enumerate(values):
            ref[pl.ds(pl.multiple_of(group * (rows * 8) + n * 8, 8), 8), :] = value

    def prepare(group, carry):
        first = group * 48
        place = [state_ref[pl.ds(first + c, 8, stride=6), :] - ORIGIN[c] for c in range(3)]
        speed = [state_ref[pl.ds(first + 3 + c, 8, stride=6), :] for c in range(3)]
        norm = place[0] * place[0] + place[1] * place[1] + place[2] * place[2]
        norm = pieces(-scale * norm, 3)
        left, right, slide = [], [], []
        for c in range(3):
            p1, p2, p3 = pieces(place[c], 3)
            q1, q2, q3 = pieces(place[c] * (2.0 * scale), 3)
            left += [p1, p1, p2, p2, p1, p3]
            right += [q1, q2, q1, q2, q3, q1]
        left += norm + [one] * 3
        right += [one] * 3 + norm
        for c in range(3):
            slide += pieces(CONTACT_STIFF * place[c] - CONTACT_DAMP * speed[c], 3)
        slide += [one] + [pad] * 6
        put(left_ref, 24, group, left)
        put(right_ref, 24, group, right)
        put(slide_ref, 16, group, slide)
        return carry

    lax.fori_loop(0, SLOTS // 8, prepare, 0)
    acc_ref[...] = jnp.zeros_like(acc_ref)
    total = count_ref[0]

    def rows(ref, count, slot):
        return ref[pl.ds((slot >> 3) * (count * 8) + (slot & 7), count, stride=8), :]

    def batch(step, carry):
        chosen = []
        for n in range(PAIR_UNROLL):
            flat = step * PAIR_UNROLL + n
            in_range = flat < total
            at = jnp.minimum(flat, SLOTS - 1)
            i = jnp.where(in_range, pairs_ref[0, at], 0)
            j = jnp.where(in_range, pairs_ref[1, at], 0)
            chosen.append((i, j, jnp.where(in_range, i, SLOTS), jnp.where(in_range, j, SLOTS)))
        weights = []
        for i, j, _, _ in chosen:
            left = jnp.concatenate([rows(left_ref, 24, i), pad], axis=0)
            right = jnp.concatenate([rows(right_ref, 24, j), pad], axis=0).astype(BF16)
            exponent = jnp.dot(left.T.astype(BF16), right, preferred_element_type=F32)
            weights.append(jnp.exp2(exponent))
        sums = []
        for (i, j, _, _), weight in zip(chosen, weights):
            slide_i = rows(slide_ref, 16, i).astype(BF16)
            slide_j = rows(slide_ref, 16, j).astype(BF16)
            high, low = halves(weight)
            to_i = lax.dot_general(
                jnp.concatenate([high, low], axis=1),
                jnp.concatenate([slide_j, slide_j], axis=1),
                ACROSS,
                preferred_element_type=F32,
            ).T
            to_j = lax.dot_general(
                jnp.concatenate([slide_i, slide_i], axis=1),
                jnp.concatenate([high, low], axis=0),
                DOWN,
                preferred_element_type=F32,
            )
            sums.append((to_i, to_j))
        for (_, _, i, j), (to_i, to_j) in zip(chosen, sums):
            rows_i = pl.ds(pl.multiple_of(i * 16, 16), 16)
            acc_ref[rows_i, :] += to_i
            rows_j = pl.ds(pl.multiple_of(j * 16, 16), 16)
            acc_ref[rows_j, :] += to_j
        return carry

    lax.fori_loop(0, (total + PAIR_UNROLL - 1) // PAIR_UNROLL, batch, 0)

    def finish(group, carry):
        def acc(n):
            return acc_ref[pl.ds(group * 128 + n, 8, stride=16), :]

        def slide(n):
            return slide_ref[pl.ds(pl.multiple_of(group * 128 + n * 8, 8), 8), :]

        total_weight = acc(9)
        for c in range(3):
            own = slide(3 * c) + slide(3 * c + 1) + slide(3 * c + 2)
            other = acc(3 * c) + acc(3 * c + 1) + acc(3 * c + 2)
            out_ref[pl.ds(group * 24 + c, 8, stride=3), :] = own * total_weight - other
        return carry

    lax.fori_loop(0, SLOTS // 8, finish, 0)


def contact_forces(pair_count, pair_list, state):
    vmem = pl.BlockSpec(memory_space=pltpu.VMEM)
    smem = pl.BlockSpec(memory_space=pltpu.SMEM)
    return pl.pallas_call(
        contact_kernel,
        out_shape=jax.ShapeDtypeStruct((SLOTS * 3, BLK), F32),
        in_specs=[smem, smem, vmem],
        out_specs=vmem,
        scratch_shapes=[
            pltpu.VMEM((SLOTS * 24, BLK), F32),
            pltpu.VMEM((SLOTS * 24, BLK), F32),
            pltpu.VMEM((SLOTS * 16, BLK), F32),
            pltpu.VMEM(((SLOTS + 1) * 16, BLK), F32),
        ],
        compiler_params=pltpu.CompilerParams(vmem_limit_bytes=24 * MIB),
        name="contact_forces",
    )(pair_count, pair_list, state)


TILE_UNROLL = 16
TILES = 4


def bond_kernel(
    first_grain,
    grains,
    tiles_ref,
    disp_ref,
    words_ref,
    out_ref,
    base_ref,
    other_ref,
    fixed_ref,
    rest_ref,
    inverse_rest_ref,
    flag_ref,
    dead_ref,
    acc_ref,
    list_ref,
):
    lane = lane_iota((8, BLK))
    sub = sublane_iota((8, BLK))
    one = jnp.ones((8, BLK), F32)
    zero = jnp.zeros((8, BLK), F32)

    def lattice(a, c):
        index = lane + a * BLK
        return ((index & 7, (index >> 3) & 7, index >> 6)[c]).astype(F32) - ORIGIN[c]

    count = jnp.int32(0)
    for grain in range(grains):
        for t in range(TILES):
            apart = tiles_ref[t, 0, first_grain + grain] - tiles_ref[t, 1, first_grain + grain]
            list_ref[count] = grain * TILES + t
            count += jnp.where((apart >= -REACH) & (apart <= REACH), 1, 0)

    for a in range(NB):
        rows = jnp.where(sub < 6, 0.0, 1.0)
        for c in range(3):
            rows = jnp.where((sub == c) | (sub == c + 3), -2.0 * lattice(a, c), rows)
        fixed_ref[a * 8 : a * 8 + 8, :] = rows

    col_y = (lane >> 3) & 7
    for apart in range(-REACH, REACH + 1):
        for r in range(16):
            dx = sub - (lane & 7)
            dy = (r & 7) - col_y
            dz = (r >> 3) - (lane >> 6) - 2 * apart
            square = dx * dx + dy * dy + dz * dz
            near = (square >= 1) & (square <= 9)
            row = ((apart + REACH) * 16 + r) * 8
            rest = square.astype(F32)
            rest_ref[row : row + 8, :] = rest
            inverse_rest_ref[row : row + 8, :] = lax.rsqrt(jnp.maximum(rest, 1.0))
            flag_ref[row : row + 8, :] = jnp.where(near, jnp.left_shift(1, lane & 7), 0)
            dead_ref[row : row + 8, :] = jnp.where(near, 0, 1)

    for group in range(grains // 8):
        these = pl.ds(first_grain + 8 * group, 8)
        for a in range(NB):
            high, low, growth = [], [], None
            for c in range(3):
                u1, u2 = pieces(disp_ref[c, these, a * BLK : (a + 1) * BLK], 2)
                high.append(u1)
                low.append(u2)
                both = u1 + u2
                term = both * (2.0 * lattice(a, c) + both)
                growth = term if growth is None else growth + term
            g1, g2, g3 = pieces(growth, 3)
            minus_high = [-2.0 * v for v in high]
            minus_low = [-2.0 * v for v in low]
            row = (group * NB + a) * 80
            for n, value in enumerate([one, g3] + high + low + [g1, g2]):
                base_ref[row + n * 8 : row + n * 8 + 8, :] = value
            row = (group * NB + a) * 104
            for n, value in enumerate([g3, one] + minus_high + minus_low + minus_high + [zero, zero]):
                other_ref[row + n * 8 : row + n * 8 + 8, :] = value

    acc_ref[...] = jnp.zeros_like(acc_ref)

    tile_row = sublane_iota((BLK, BLK))
    tile_col = lane_iota((BLK, BLK))
    spread = jnp.where((tile_row & 15) == (tile_col >> 3), 1.0, 0.0).astype(BF16)
    own_lane = (lane >> 4) == sub

    def batch(step, carry):
        chosen = []
        for n in range(TILE_UNROLL):
            flat = step * TILE_UNROLL + n
            in_range = flat < count
            tile = list_ref[jnp.where(in_range, flat, 0)]
            grain, t = tile >> 2, tile & 3
            a = tiles_ref[t, 0, first_grain + grain]
            b = tiles_ref[t, 1, first_grain + grain]
            target = jnp.where(in_range, grain * NB + a, grains * NB)
            chosen.append((grain, t, a, b, target))

        def rows(ref, per, grain, a, first):
            start = ((grain >> 3) * NB + a) * (per * 8) + first * 8 + (grain & 7)
            return ref[pl.ds(start, 8, stride=8), :]

        def fixed(a):
            return fixed_ref[pl.ds(pl.multiple_of(a * 8, 8), 8), :]

        growths, words = [], []
        for grain, t, a, b, _ in chosen:
            base_a = rows(base_ref, 10, grain, a, 2)
            left = jnp.concatenate([base_a, fixed(a), rows(base_ref, 10, grain, a, 0), base_a], axis=0)
            right = jnp.concatenate(
                [
                    fixed(b),
                    rows(base_ref, 10, grain, b, 2),
                    rows(other_ref, 13, grain, b, 0),
                    rows(other_ref, 13, grain, b, 5),
                ],
                axis=0,
            ).astype(BF16)
            growths.append(jnp.dot(left.T.astype(BF16), right, preferred_element_type=F32))
            word = words_ref[pl.ds((first_grain + grain) * 64 + t, 16, stride=4), :].astype(F32)
            picked = jnp.concatenate(
                [jnp.where(own_lane, jnp.broadcast_to(word[r : r + 1, :], (8, BLK)), 0.0) for r in range(16)],
                axis=0,
            ).astype(BF16)
            words.append(jnp.dot(picked, spread, preferred_element_type=F32).astype(jnp.int32))
        pulls = []
        for (grain, t, a, b, _), growth, word in zip(chosen, growths, words):
            apart = jnp.clip(b - a, -REACH, REACH) + REACH
            table = pl.ds(pl.multiple_of(apart * BLK, BLK), BLK)
            live = (word & flag_ref[table, :]) == dead_ref[table, :]
            pull = inverse_rest_ref[table, :] - lax.rsqrt(rest_ref[table, :] + growth)
            pulls.append(jnp.where(live, pull, 0.0))
        forces = []
        for (grain, t, a, b, _), pull in zip(chosen, pulls):
            high, low = halves(pull)
            moments = jnp.concatenate([rows(base_ref, 10, grain, b, 2), fixed(b)], axis=0).astype(BF16)
            forces.append(
                lax.dot_general(
                    jnp.concatenate([high, low], axis=1),
                    jnp.concatenate([moments, moments], axis=1),
                    ACROSS,
                    preferred_element_type=F32,
                ).T
            )
        for (_, _, _, _, target), force in zip(chosen, forces):
            acc_ref[pl.ds(pl.multiple_of(target * 16, 16), 16), :] += force
        return carry

    lax.fori_loop(0, (count + TILE_UNROLL - 1) // TILE_UNROLL, batch, 0)

    for group in range(grains // 8):
        for a in range(NB):
            row = (group * 8 * NB + a) * 16
            acc = [acc_ref[pl.ds(row + n, 8, stride=NB * 16), :] for n in (0, 1, 2, 3, 4, 5, 8, 9, 10, 14)]
            base = (group * NB + a) * 80
            for c in range(3):
                own = lattice(a, c) + (
                    base_ref[base + 16 + 8 * c : base + 24 + 8 * c, :]
                    + base_ref[base + 40 + 8 * c : base + 48 + 8 * c, :]
                )
                force = acc[c] + acc[3 + c] - 0.5 * acc[6 + c] - acc[9] * own
                out_ref[c, 8 * group : 8 * group + 8, a * BLK : (a + 1) * BLK] = force * BOND_STIFF


def bond_forces(first_grain, grains, tile_list, displacement, words):
    vmem = pl.BlockSpec(memory_space=pltpu.VMEM)
    smem = pl.BlockSpec(memory_space=pltpu.SMEM)
    blocks = grains * NB
    table = (2 * REACH + 1) * BLK
    return pl.pallas_call(
        functools.partial(bond_kernel, first_grain, grains),
        out_shape=jax.ShapeDtypeStruct((3, grains, NODES), F32),
        in_specs=[smem, vmem, vmem],
        out_specs=vmem,
        scratch_shapes=[
            pltpu.VMEM((blocks * 10, BLK), F32),
            pltpu.VMEM((blocks * 13, BLK), F32),
            pltpu.VMEM((NB * 8, BLK), F32),
            pltpu.VMEM((table, BLK), F32),
            pltpu.VMEM((table, BLK), F32),
            pltpu.VMEM((table, BLK), jnp.int32),
            pltpu.VMEM((table, BLK), jnp.int32),
            pltpu.VMEM(((blocks + 1) * 16, BLK), F32),
            pltpu.SMEM((grains * TILES + 1,), jnp.int32),
        ],
        compiler_params=pltpu.CompilerParams(vmem_limit_bytes=24 * MIB),
        cost_estimate=pl.CostEstimate(flops=2_000_000_000, transcendentals=2_000_000, bytes_accessed=2_000_000),
        name="bond_forces",
    )(tile_list, displacement, words)


def inverse_kernel(nodes_ref, out_ref):
    sub128 = sublane_iota((BLK, SB * BLK))
    sub16 = sublane_iota((16, SB * BLK))
    k_index = lane_iota((16, SB * BLK))
    k_value = jnp.where(sub16 < 8, k_index & 127, 1 + (k_index >> 7)).astype(F32)

    def step(part, carry):
        for n in range(8):
            grain = part * 8 + n
            node = nodes_ref[pl.ds(grain, 1), :]
            hit = jnp.where(jnp.broadcast_to(node & 127, (BLK, SB * BLK)) == sub128, 1.0, 0.0).astype(BF16)
            block = jnp.broadcast_to(node >> 7, (16, SB * BLK))
            value = jnp.where(block == (sub16 & 7), k_value, 0.0).astype(BF16)
            out_ref[pl.ds(pl.multiple_of(grain * 16, 16), 16), :] = lax.dot_general(
                value, hit, ACROSS, preferred_element_type=F32
            )
        return carry

    lax.fori_loop(0, GRAINS_DEV // 8, step, 0)


def surface_places(surface_nodes):
    vmem = pl.BlockSpec(memory_space=pltpu.VMEM)
    return pl.pallas_call(
        inverse_kernel,
        out_shape=jax.ShapeDtypeStruct((GRAINS_DEV * 16, BLK), F32),
        in_specs=[vmem],
        out_specs=vmem,
        compiler_params=pltpu.CompilerParams(vmem_limit_bytes=8 * MIB),
        cost_estimate=pl.CostEstimate(flops=500_000_000, transcendentals=0, bytes_accessed=500_000),
        name="surface_places",
    )(surface_nodes)


def sum_kernel(bonds, send_ref, back_ref, inverse_ref, vel_ref, *refs):
    bond_refs, (force_ref, new_ref, block_ref) = refs[:bonds], refs[bonds:]
    for d in range(SLOTS):
        block = send_ref[0, d]
        grain = block >> 2
        row = ((grain >> 3) * SB + (block & 3)) * 24 + (grain & 7)
        block_ref[pl.ds(row, 3, stride=8), :] = back_ref[3 * d : 3 * d + 3, :]
    for group in range(GROUPS):
        grains = pl.ds(8 * group, 8)
        bond_ref = bond_refs[group * bonds // GROUPS]
        bond_grains = pl.ds((8 * group) % (GRAINS_DEV // bonds), 8)
        for a in range(NB):
            lane = inverse_ref[pl.ds(group * 128 + a, 8, stride=16), :].astype(jnp.int32)
            block = inverse_ref[pl.ds(group * 128 + 8 + a, 8, stride=16), :].astype(jnp.int32)
            columns = slice(a * BLK, (a + 1) * BLK)
            for c in range(3):
                value = jnp.zeros((8, BLK), F32)
                for k in range(SB):
                    start = (group * SB + k) * 24 + c * 8
                    value = jnp.where(block == k + 1, lane_gather(block_ref[start : start + 8, :], lane), value)
                force = bond_ref[c, bond_grains, columns] + value
                force_ref[c, grains, columns] = force
                new_ref[c, grains, columns] = vel_ref[c, grains, columns] + TIME_STEP * force


def sum_forces(send_order, returned, inverse, velocity, bonds):
    vmem = pl.BlockSpec(memory_space=pltpu.VMEM)
    shape = jax.ShapeDtypeStruct((3, GRAINS_DEV, NODES), F32)
    return pl.pallas_call(
        functools.partial(sum_kernel, len(bonds)),
        out_shape=(shape, shape),
        in_specs=[pl.BlockSpec(memory_space=pltpu.SMEM)] + [vmem] * (3 + len(bonds)),
        out_specs=(vmem, vmem),
        scratch_shapes=[pltpu.VMEM((SLOTS * 3, BLK), F32)],
        compiler_params=pltpu.CompilerParams(vmem_limit_bytes=8 * MIB),
        name="sum_forces",
    )(send_order, returned, inverse, velocity, *bonds)


def exchange(rows, width):
    moved = lax.all_to_all(
        rows.reshape(SLOTS, 1, width, BLK), ("grain", "cell"), split_axis=0, concat_axis=0, tiled=True
    )
    return moved.reshape(SLOTS * width, BLK)


def on_device(
    displacement,
    velocity,
    centers,
    tile_list,
    broken_bits,
    surface_nodes,
    send_order,
    pair_list,
    pair_count,
):
    displacement = displacement.transpose(1, 0, 2)
    velocity = velocity.transpose(1, 0, 2)
    tiles = tile_list.transpose(1, 2, 0)
    pairs = pair_list[0].T
    words = broken_bits.reshape(GRAINS_DEV, TILES, 16, BLK).transpose(0, 2, 1, 3).reshape(GRAINS_DEV * 64, BLK)
    outgoing = surface_blocks(send_order, displacement, velocity, centers, surface_nodes)
    received = exchange(outgoing, 6)
    half = GRAINS_DEV // 2
    bonds = [bond_forces(first, half, tiles, displacement, words) for first in (0, half)]
    inverse = surface_places(surface_nodes)
    received, bonds[0] = lax.optimization_barrier((received, bonds[0]))
    slot_force = contact_forces(pair_count, pairs, received)
    returned = exchange(slot_force, 3)
    force, new_velocity = sum_forces(send_order, returned, inverse, velocity, bonds)
    return force.transpose(1, 0, 2), new_velocity.transpose(1, 0, 2)


def solution(mesh):
    return jax.shard_map(
        on_device,
        mesh=mesh,
        in_specs=(
            P(("grain", "cell"), None, None),
            P(("grain", "cell"), None, None),
            P(None, ("grain", "cell")),
            P(("grain", "cell"), None, None),
            P(("grain", "cell"), None, None),
            P(("grain", "cell"), None),
            P(("grain", "cell"), None),
            P(("grain", "cell"), None, None),
            P(("grain", "cell")),
        ),
        out_specs=(P(("grain", "cell"), None, None), P(("grain", "cell"), None, None)),
        check_vma=False,
    )
```

profile of v0, /device:TPU:1, one launch (start us, length us, event | category | flops | bytes accessed | tf_op | source)
XLA Modules:
  0.0 56.0 jit_solution(8445049182835191837)
XLA Ops:
  0.6 0.0 copy-start.6
  0.6 0.0 copy-start.7
  0.7 0.7 %copy-done.6 = f32[3,32]{1,0:T(4,128)S(1)} copy-done((f32[3,32]{1,0:T(4,128)S(1)}, f32[3,32]{1,0:T(4,128)}, u32[]{:S(2)}) %copy-start.6) | copy-done | bytes 408
  1.3 0.0 copy-done.7
  1.3 1.0 %copy-done = f32[32,3,768]{2,0,1:T(8,128)S(1)} copy-done((f32[32,3,768]{2,0,1:T(8,128)S(1)}, f32[32,3,768]{2,0,1:T(8,128)}, u32[]{:S(2)}) %copy-start) | copy-done | bytes 294936
  2.3 1.0 %copy-done.2 = f32[32,3,768]{2,0,1:T(8,128)S(1)} copy-done((f32[32,3,768]{2,0,1:T(8,128)S(1)}, f32[32,3,768]{2,0,1:T(8,128)}, u32[]{:S(2)}) %copy-start.2) | copy-done | bytes 294936
  3.2 0.8 %copy-done.4 = s32[32,512]{1,0:T(8,128)S(1)} copy-done((s32[32,512]{1,0:T(8,128)S(1)}, s32[32,512]{1,0:T(8,128)}, u32[]{:S(2)}) %copy-start.4) | copy-done | bytes 65560
  4.1 2.4 %surface_blocks.1 = f32[768,128]{1,0:T(8,128)} custom-call(s32[1,128]{1,0:T(1,128)S(1)} %copy-done.7, f32[3,32,768]{2,1,0:T(8,128)S(1)} %bitcast.21, f32[3,32,768]{2,1,0:T(8,128)S(1)} %bitcast.18, f32[3,32]{1,0:T(4,128)S(1)} %copy-done.6, s32[32,512]{1,0:T(8,128)S(1)} %copy-done.4), custom_call_target="tpu_custom_call" | custom-call | tf_op jit(solution)/shard_map/surface_blocks/pallas_call | solution.py:98
  6.5 11.5 %all-to-all-start = ((f32[128,1,6,128]{3,1,2,0:T(1,128)}), f32[128,1,6,128]{3,1,2,0:T(1,128)S(1)}, u32[]{:S(2)}, u32[]{:S(2)}) async-start(f32[128,1,6,128]{3,1,2,0:T(1,128)} %bitcast.4), calls=%async_computation | async-start | bytes 786432 | tf_op jit(solution)/shard_map/all_to_all | solution.py:493
  18.0 0.0 copy-start.10
  18.7 0.0 copy-done.9
  18.7 0.0 copy-done.3
  18.7 0.0 copy-done.10
  18.7 4.2 %bond_forces.2.refs_0_ = f32[3,16,768]{2,1,0:T(8,128)S(1)} custom-call(s32[4,2,32]{2,1,0:T(2,128)S(1)} %bitcast.27, f32[3,32,768]{2,1,0:T(8,128)S(1)} %bitcast.22, s32[2048,128]{1,0:T(8,128)S(1)} %bitcast.25), custom_call_target="tpu_custom_call" | custom-call | flops 2000000000 | bytes 2000000 | tf_op jit(solution)/shard_map/bond_forces/pallas_call | solution.py:397
  22.9 7.8 %all-to-all-done = f32[128,1,6,128]{3,1,2,0:T(1,128)S(1)} async-done(((f32[128,1,6,128]{3,1,2,0:T(1,128)}), f32[128,1,6,128]{3,1,2,0:T(1,128)S(1)}, u32[]{:S(2)}, u32[]{:S(2)}) %all-to-all-start) | async-done | bytes 393248 | tf_op jit(solution)/shard_map/all_to_all | solution.py:493
  30.7 0.7 %copy-done.8 = s32[1,128,2]{1,2,0:T(2,128)S(1)} copy-done((s32[1,128,2]{1,2,0:T(2,128)S(1)}, s32[1,128,2]{1,2,0:T(2,128)}, u32[]{:S(2)}) %copy-start.8) | copy-done | bytes 1048
  31.4 4.2 %contact_forces.1 = f32[384,128]{1,0:T(8,128)} custom-call(s32[1]{0:T(128)S(6)} %copy.16.count_ref, s32[2,128]{1,0:T(2,128)S(1)} %bitcast.24, f32[768,128]{1,0:T(8,128)S(1)} %bitcast.17), custom_call_target="tpu_custom_call" | custom-call | tf_op jit(solution)/shard_map/contact_forces/pallas_call | solution.py:212
  35.6 7.6 %all-to-all-start.1 = ((f32[128,1,3,128]{3,1,2,0:T(1,128)}), f32[128,1,3,128]{3,1,2,0:T(1,128)S(1)}, u32[]{:S(2)}, u32[]{:S(2)}) async-start(f32[128,1,3,128]{3,1,2,0:T(1,128)} %bitcast.10), calls=%async_computation.1 | async-start | bytes 393216 | tf_op jit(solution)/shard_map/all_to_all | solution.py:493
  43.2 0.0 copy-done.5
  43.2 1.6 %surface_places.1.inverse_ref = f32[512,128]{1,0:T(8,128)S(1)} custom-call(s32[32,512]{1,0:T(8,128)S(1)} %copy-done.5), custom_call_target="tpu_custom_call" | custom-call | flops 500000000 | bytes 500000 | tf_op jit(solution)/shard_map/surface_places/pallas_call | solution.py:442
  44.8 4.2 %bond_forces.3.refs_1_ = f32[3,16,768]{2,1,0:T(8,128)S(1)} custom-call(s32[4,2,32]{2,1,0:T(2,128)S(1)} %bitcast.28, f32[3,32,768]{2,1,0:T(8,128)S(1)} %bitcast.23, s32[2048,128]{1,0:T(8,128)S(1)} %bitcast.26), custom_call_target="tpu_custom_call" | custom-call | flops 2000000000 | bytes 2000000 | tf_op jit(solution)/shard_map/bond_forces/pallas_call | solution.py:397
  49.0 4.8 %all-to-all-done.1 = f32[128,1,3,128]{3,1,2,0:T(1,128)S(1)} async-done(((f32[128,1,3,128]{3,1,2,0:T(1,128)}), f32[128,1,3,128]{3,1,2,0:T(1,128)S(1)}, u32[]{:S(2)}, u32[]{:S(2)}) %all-to-all-start.1) | async-done | bytes 196640 | tf_op jit(solution)/shard_map/all_to_all | solution.py:493
  53.8 0.0 copy-done.1
  53.8 2.2 %sum_forces.1 = (f32[3,32,768]{2,1,0:T(8,128)}, f32[3,32,768]{2,1,0:T(8,128)}) custom-call(s32[1,128]{1,0:T(1,128)S(1)} %copy-done.7, f32[384,128]{1,0:T(8,128)S(1)} %bitcast.20, f32[512,128]{1,0:T(8,128)S(1)} %surface_places.1.inverse_ref, f32[3,32,768]{2,1,0:T(8,128)S(1)} %bitcast.19, f32[3,16,768]{2,1,0:T(8,128)S(1)} %bond_forces.2.refs_0_, ...), custom_call_target="tpu_custom_call" | custom-call | tf_op jit(solution)/shard_map/sum_forces/pallas_call | solution.py:481
  (8 shorter events, 0.0 us)
Async XLA Ops:
  0.6 0.7 %copy-start.6 = (f32[3,32]{1,0:T(4,128)S(1)}, f32[3,32]{1,0:T(4,128)}, u32[]{:S(2)}) copy-start(f32[3,32]{1,0:T(4,128)} %centers_ref.1) | copy-start | bytes 1156
  0.6 0.7 %copy-start.7 = (s32[1,128]{1,0:T(1,128)S(1)}, s32[1,128]{1,0:T(1,128)}, u32[]{:S(2)}) copy-start(s32[1,128]{1,0:T(1,128)} %send_ref.3) | copy-start | bytes 1540
  1.3 1.0 %copy-start = (f32[32,3,768]{2,0,1:T(8,128)S(1)}, f32[32,3,768]{2,0,1:T(8,128)}, u32[]{:S(2)}) copy-start(f32[32,3,768]{2,0,1:T(8,128)} %param.10) | copy-start | bytes 884740
  2.3 1.0 %copy-start.2 = (f32[32,3,768]{2,0,1:T(8,128)S(1)}, f32[32,3,768]{2,0,1:T(8,128)}, u32[]{:S(2)}) copy-start(f32[32,3,768]{2,0,1:T(8,128)} %param.9) | copy-start | bytes 884740
  3.2 0.8 %copy-start.4 = (s32[32,512]{1,0:T(8,128)S(1)}, s32[32,512]{1,0:T(8,128)}, u32[]{:S(2)}) copy-start(s32[32,512]{1,0:T(8,128)} %nodes_ref.3) | copy-start | bytes 196612
  4.1 14.6 %copy-start.9 = (s32[32,4,2048]{2,1,0:T(4,128)S(1)}, s32[32,4,2048]{2,1,0:T(4,128)}, u32[]{:S(2)}) copy-start(s32[32,4,2048]{2,1,0:T(4,128)} %param.13) | copy-start | bytes 3145732
  6.5 12.2 %copy-start.3 = (f32[32,3,768]{2,0,1:T(8,128)S(1)}, f32[32,3,768]{2,0,1:T(8,128)}, u32[]{:S(2)}) copy-start(f32[32,3,768]{2,0,1:T(8,128)} %param.9) | copy-start | bytes 884740
  6.5 24.2 %all-to-all-start = ((f32[128,1,6,128]{3,1,2,0:T(1,128)}), f32[128,1,6,128]{3,1,2,0:T(1,128)S(1)}, u32[]{:S(2)}, u32[]{:S(2)}) async-start(f32[128,1,6,128]{3,1,2,0:T(1,128)} %bitcast.4), calls=%async_computation | async-start | bytes 786432 | tf_op jit(solution)/shard_map/all_to_all | solution.py:493
  18.0 0.7 %copy-start.10 = (s32[32,4,2]{0,2,1:T(2,128)S(1)}, s32[32,4,2]{0,2,1:T(2,128)}, u32[]{:S(2)}) copy-start(s32[32,4,2]{0,2,1:T(2,128)} %param.12) | copy-start | bytes 3076
  30.7 0.7 %copy-start.8 = (s32[1,128,2]{1,2,0:T(2,128)S(1)}, s32[1,128,2]{1,2,0:T(2,128)}, u32[]{:S(2)}) copy-start(s32[1,128,2]{1,2,0:T(2,128)} %param.16) | copy-start | bytes 3076
  35.6 7.6 %copy-start.5 = (s32[32,512]{1,0:T(8,128)S(1)}, s32[32,512]{1,0:T(8,128)}, u32[]{:S(2)}) copy-start(s32[32,512]{1,0:T(8,128)} %nodes_ref.3) | copy-start | bytes 196612
  35.6 18.2 %all-to-all-start.1 = ((f32[128,1,3,128]{3,1,2,0:T(1,128)}), f32[128,1,3,128]{3,1,2,0:T(1,128)S(1)}, u32[]{:S(2)}, u32[]{:S(2)}) async-start(f32[128,1,3,128]{3,1,2,0:T(1,128)} %bitcast.10), calls=%async_computation.1 | async-start | bytes 393216 | tf_op jit(solution)/shard_map/all_to_all | solution.py:493
  44.8 9.0 %copy-start.1 = (f32[32,3,768]{2,0,1:T(8,128)S(1)}, f32[32,3,768]{2,0,1:T(8,128)}, u32[]{:S(2)}) copy-start(f32[32,3,768]{2,0,1:T(8,128)} %param.10) | copy-start | bytes 884740
where the time goes:
time: 56.4 us; the launch traced here: 56 us
  starting transfers between devices  19 us (34%)
  Pallas kernels  18.8 us (33%)
  waiting for transfers between devices  12.6 us (22%)
  local copies, waits for them, and re-layouts  4.13 us (7%)
  between operations  1.38 us (2%)
    all_to_all x2, starting transfers between devices, exchange(): lax.all_to_all(rows.reshape(SLOTS, 1, width, BLK), ('grain', 'cell'), spl...  19 us
    all_to_all x2, waiting for transfers between devices, exchange(): lax.all_to_all(rows.reshape(SLOTS, 1, width, BLK), ('grain', 'cell'), spl...  12.6 us
    pallas_call x2, Pallas kernels, bond_forces(): pl.pallas_call(functools.partial(bond_kernel, first_grain, grains), out_s...  8.37 us
    pallas_call x1, Pallas kernels, contact_forces(): pl.pallas_call(contact_kernel, out_shape=jax.ShapeDtypeStruct((SLOTS * 3,...  4.23 us
    unnamed x22, local copies, waits for them, and re-layouts  4.13 us
    pallas_call x1, Pallas kernels, surface_blocks(): pl.pallas_call(gather_kernel, out_shape=jax.ShapeDtypeStruct((SLOTS * 6,...  2.44 us
    pallas_call x1, Pallas kernels, sum_forces(): pl.pallas_call(functools.partial(sum_kernel, len(bonds)), out_shape=(shap...  2.16 us
    pallas_call x1, Pallas kernels, surface_places(): pl.pallas_call(inverse_kernel, out_shape=jax.ShapeDtypeStruct((GRAINS_DEV...  1.56 us
  transfers between devices with their start and end apart: 2, of which 2 were waited for; matrix products, arithmetic and copies ran while one was open for 0% of the time, Pallas kernels for 18%

commit v1 on v0

--- a/solution.py
+++ b/solution.py
@@ -30,6 +30,7 @@
 REACH = 2
 ACROSS = (((1,), (1,)), ((), ()))
 DOWN = (((1,), (0,)), ((), ()))
+ALONG = (((0,), (0,)), ((), ()))
 
 
 def pieces(value, count):
@@ -60,7 +61,44 @@
     return lax.broadcasted_iota(jnp.int32, shape, 0)
 
 
-def gather_kernel(send_ref, disp_ref, vel_ref, centers_ref, nodes_ref, out_ref, state_ref):
+def gather_kernel(
+    send_hbm,
+    disp_hbm,
+    vel_hbm,
+    centers_hbm,
+    nodes_hbm,
+    out_hbm,
+    send_ref,
+    disp_ref,
+    vel_ref,
+    centers_ref,
+    nodes_ref,
+    state_ref,
+    out_ref,
+    sems,
+    group_sems,
+    out_sems,
+):
+    small = [
+        pltpu.make_async_copy(centers_hbm, centers_ref, sems.at[0]),
+        pltpu.make_async_copy(send_hbm, send_ref, sems.at[1]),
+    ]
+    large = []
+    for group in range(GROUPS):
+        these = pl.ds(8 * group, 8)
+        large.append(
+            [
+                pltpu.make_async_copy(nodes_hbm.at[these], nodes_ref.at[these], group_sems.at[group, 0]),
+                pltpu.make_async_copy(disp_hbm.at[:, these], disp_ref.at[:, these], group_sems.at[group, 1]),
+                pltpu.make_async_copy(vel_hbm.at[:, these], vel_ref.at[:, these], group_sems.at[group, 2]),
+            ]
+        )
+    small[0].start()
+    for copies in large:
+        for copy in copies:
+            copy.start()
+    small[1].start()
+    small[0].wait()
     for group in range(GROUPS):
         grains = pl.ds(8 * group, 8)
         own = lane_iota((8, GRAINS_DEV)) == sublane_iota((8, GRAINS_DEV)) + 8 * group
@@ -72,6 +110,8 @@
             )
             for c in range(3)
         ]
+        for copy in large[group]:
+            copy.wait()
         for k in range(SB):
             node = nodes_ref[grains, k * BLK : (k + 1) * BLK]
             lane = node & (BLK - 1)
@@ -86,30 +126,63 @@
                 if c < 3:
                     value = rest[c].astype(F32) + value + offsets[c]
                 state_ref[pl.ds((group * SB + k) * 48 + c * 8, 8), :] = value
+    small[1].wait()
+    done = []
     for d in range(SLOTS):
         block = send_ref[0, d]
         grain = block >> 2
         row = ((grain >> 3) * SB + (block & 3)) * 48 + (grain & 7)
         out_ref[6 * d : 6 * d + 6, :] = state_ref[pl.ds(row, 6, stride=8), :]
+        if d % 32 == 31:
+            part = pl.ds(6 * (d - 31), 192)
+            done.append(pltpu.make_async_copy(out_ref.at[part], out_hbm.at[part], out_sems.at[d // 32]))
+            done[-1].start()
+    for copy in done:
+        copy.wait()
 
 
 def surface_blocks(send_order, displacement, velocity, centers, surface_nodes):
-    vmem = pl.BlockSpec(memory_space=pltpu.VMEM)
+    hbm = pl.BlockSpec(memory_space=pltpu.HBM)
     return pl.pallas_call(
         gather_kernel,
         out_shape=jax.ShapeDtypeStruct((SLOTS * 6, BLK), F32),
-        in_specs=[pl.BlockSpec(memory_space=pltpu.SMEM), vmem, vmem, vmem, vmem],
-        out_specs=vmem,
-        scratch_shapes=[pltpu.VMEM((SLOTS * 6, BLK), F32)],
-        compiler_params=pltpu.CompilerParams(vmem_limit_bytes=8 * MIB),
+        in_specs=[hbm] * 5,
+        out_specs=hbm,
+        scratch_shapes=[
+            pltpu.SMEM((1, SLOTS), jnp.int32),
+            pltpu.VMEM((3, GRAINS_DEV, NODES), F32),
+            pltpu.VMEM((3, GRAINS_DEV, NODES), F32),
+            pltpu.VMEM((3, GRAINS_DEV), F32),
+            pltpu.VMEM((GRAINS_DEV, SB * BLK), jnp.int32),
+            pltpu.VMEM((SLOTS * 6, BLK), F32),
+            pltpu.VMEM((SLOTS * 6, BLK), F32),
+            pltpu.SemaphoreType.DMA((2,)),
+            pltpu.SemaphoreType.DMA((GROUPS, 3)),
+            pltpu.SemaphoreType.DMA((GROUPS,)),
+        ],
+        compiler_params=pltpu.CompilerParams(vmem_limit_bytes=60 * MIB),
         name="surface_blocks",
     )(send_order, displacement, velocity, centers, surface_nodes)
 
 
-PAIR_UNROLL = 16
-
-
-def contact_kernel(count_ref, pairs_ref, state_ref, out_ref, left_ref, right_ref, slide_ref, acc_ref):
+PAIR_UNROLL = 32
+
+
+def contact_kernel(
+    lists_hbm,
+    state_ref,
+    out_hbm,
+    lists_ref,
+    left_ref,
+    right_ref,
+    slide_ref,
+    acc_ref,
+    out_ref,
+    sem,
+    out_sems,
+):
+    fetch = pltpu.make_async_copy(lists_hbm, lists_ref, sem)
+    fetch.start()
     scale = math.log2(math.e) / CONTACT_RANGE
     one = jnp.ones((8, BLK), F32)
     pad = jnp.zeros((8, BLK), F32)
@@ -134,15 +207,16 @@
         right += [one] * 3 + norm
         for c in range(3):
             slide += pieces(CONTACT_STIFF * place[c] - CONTACT_DAMP * speed[c], 3)
-        slide += [one] + [pad] * 6
+        slide += [one]
         put(left_ref, 24, group, left)
         put(right_ref, 24, group, right)
         put(slide_ref, 16, group, slide)
         return carry
 
-    lax.fori_loop(0, SLOTS // 8, prepare, 0)
+    lax.fori_loop(0, SLOTS // 8, prepare, 0, unroll=4)
     acc_ref[...] = jnp.zeros_like(acc_ref)
-    total = count_ref[0]
+    fetch.wait()
+    total = lists_ref[2, 0]
 
     def rows(ref, count, slot):
         return ref[pl.ds((slot >> 3) * (count * 8) + (slot & 7), count, stride=8), :]
@@ -153,29 +227,28 @@
             flat = step * PAIR_UNROLL + n
             in_range = flat < total
             at = jnp.minimum(flat, SLOTS - 1)
-            i = jnp.where(in_range, pairs_ref[0, at], 0)
-            j = jnp.where(in_range, pairs_ref[1, at], 0)
+            i = jnp.where(in_range, lists_ref[0, at], 0)
+            j = jnp.where(in_range, lists_ref[1, at], 0)
             chosen.append((i, j, jnp.where(in_range, i, SLOTS), jnp.where(in_range, j, SLOTS)))
         weights = []
         for i, j, _, _ in chosen:
-            left = jnp.concatenate([rows(left_ref, 24, i), pad], axis=0)
+            left = jnp.concatenate([rows(left_ref, 24, i), pad], axis=0).astype(BF16)
             right = jnp.concatenate([rows(right_ref, 24, j), pad], axis=0).astype(BF16)
-            exponent = jnp.dot(left.T.astype(BF16), right, preferred_element_type=F32)
+            exponent = lax.dot_general(left, right, ALONG, preferred_element_type=F32)
             weights.append(jnp.exp2(exponent))
         sums = []
         for (i, j, _, _), weight in zip(chosen, weights):
             slide_i = rows(slide_ref, 16, i).astype(BF16)
             slide_j = rows(slide_ref, 16, j).astype(BF16)
-            high, low = halves(weight)
             to_i = lax.dot_general(
-                jnp.concatenate([high, low], axis=1),
                 jnp.concatenate([slide_j, slide_j], axis=1),
-                ACROSS,
+                jnp.concatenate(halves(weight.T), axis=0),
+                DOWN,
                 preferred_element_type=F32,
-            ).T
+            )
             to_j = lax.dot_general(
                 jnp.concatenate([slide_i, slide_i], axis=1),
-                jnp.concatenate([high, low], axis=0),
+                jnp.concatenate(halves(weight), axis=0),
                 DOWN,
                 preferred_element_type=F32,
             )
@@ -189,44 +262,56 @@
 
     lax.fori_loop(0, (total + PAIR_UNROLL - 1) // PAIR_UNROLL, batch, 0)
 
-    def finish(group, carry):
+    def finish(group):
         def acc(n):
             return acc_ref[pl.ds(group * 128 + n, 8, stride=16), :]
 
         def slide(n):
-            return slide_ref[pl.ds(pl.multiple_of(group * 128 + n * 8, 8), 8), :]
+            return slide_ref[group * 128 + n * 8 : group * 128 + n * 8 + 8, :]
 
         total_weight = acc(9)
         for c in range(3):
             own = slide(3 * c) + slide(3 * c + 1) + slide(3 * c + 2)
             other = acc(3 * c) + acc(3 * c + 1) + acc(3 * c + 2)
             out_ref[pl.ds(group * 24 + c, 8, stride=3), :] = own * total_weight - other
-        return carry
-
-    lax.fori_loop(0, SLOTS // 8, finish, 0)
-
-
-def contact_forces(pair_count, pair_list, state):
+
+    done = []
+    for group in range(SLOTS // 8):
+        finish(group)
+        if group % 4 == 3:
+            part = pl.ds(24 * (group - 3), 96)
+            done.append(pltpu.make_async_copy(out_ref.at[part], out_hbm.at[part], out_sems.at[group // 4]))
+            done[-1].start()
+    for copy in done:
+        copy.wait()
+
+
+def contact_forces(lists, state):
     vmem = pl.BlockSpec(memory_space=pltpu.VMEM)
-    smem = pl.BlockSpec(memory_space=pltpu.SMEM)
+    hbm = pl.BlockSpec(memory_space=pltpu.HBM)
     return pl.pallas_call(
         contact_kernel,
         out_shape=jax.ShapeDtypeStruct((SLOTS * 3, BLK), F32),
-        in_specs=[smem, smem, vmem],
-        out_specs=vmem,
+        in_specs=[pl.BlockSpec(memory_space=pl.ANY), vmem],
+        out_specs=hbm,
         scratch_shapes=[
+            pltpu.SMEM((8, SLOTS), jnp.int32),
             pltpu.VMEM((SLOTS * 24, BLK), F32),
             pltpu.VMEM((SLOTS * 24, BLK), F32),
             pltpu.VMEM((SLOTS * 16, BLK), F32),
             pltpu.VMEM(((SLOTS + 1) * 16, BLK), F32),
+            pltpu.VMEM((SLOTS * 3, BLK), F32),
+            pltpu.SemaphoreType.DMA,
+            pltpu.SemaphoreType.DMA((4,)),
         ],
         compiler_params=pltpu.CompilerParams(vmem_limit_bytes=24 * MIB),
         name="contact_forces",
-    )(pair_count, pair_list, state)
+    )(lists, state)
 
 
 TILE_UNROLL = 16
 TILES = 4
+BOND_PARTS = ((0, 8), (8, 24))
 
 
 def bond_kernel(
@@ -416,7 +501,11 @@
     )(tile_list, displacement, words)
 
 
-def inverse_kernel(nodes_ref, out_ref):
+def inverse_kernel(count_ref, nodes_ref, pairs_ref, send_ref, out_ref, lists_ref):
+    lists_ref[:2, :] = pairs_ref[...]
+    lists_ref[2:3, :] = jnp.full((1, SLOTS), count_ref[0], jnp.int32)
+    lists_ref[3:4, :] = send_ref[...]
+    lists_ref[4:, :] = jnp.zeros((4, SLOTS), jnp.int32)
     sub128 = sublane_iota((BLK, SB * BLK))
     sub16 = sublane_iota((16, SB * BLK))
     k_index = lane_iota((16, SB * BLK))
@@ -437,33 +526,47 @@
     lax.fori_loop(0, GRAINS_DEV // 8, step, 0)
 
 
-def surface_places(surface_nodes):
+def surface_places(pair_count, surface_nodes, pairs, send_order):
     vmem = pl.BlockSpec(memory_space=pltpu.VMEM)
     return pl.pallas_call(
         inverse_kernel,
-        out_shape=jax.ShapeDtypeStruct((GRAINS_DEV * 16, BLK), F32),
-        in_specs=[vmem],
-        out_specs=vmem,
+        out_shape=(
+            jax.ShapeDtypeStruct((GRAINS_DEV * 16, BLK), F32),
+            jax.ShapeDtypeStruct((8, SLOTS), jnp.int32),
+        ),
+        in_specs=[pl.BlockSpec(memory_space=pltpu.SMEM), vmem, vmem, vmem],
+        out_specs=(vmem, vmem),
         compiler_params=pltpu.CompilerParams(vmem_limit_bytes=8 * MIB),
         cost_estimate=pl.CostEstimate(flops=500_000_000, transcendentals=0, bytes_accessed=500_000),
         name="surface_places",
-    )(surface_nodes)
-
-
-def sum_kernel(bonds, send_ref, back_ref, inverse_ref, vel_ref, *refs):
-    bond_refs, (force_ref, new_ref, block_ref) = refs[:bonds], refs[bonds:]
+    )(pair_count, surface_nodes, pairs, send_order)
+
+
+def sum_kernel(bonds, lists_hbm, back_ref, inverse_ref, vel_ref, *refs):
+    bond_refs = refs[:bonds]
+    force_hbm, new_hbm, lists_ref, force_ref, new_ref, block_ref, lists_sem, out_sems = refs[bonds:]
+    fetch = pltpu.make_async_copy(lists_hbm, lists_ref, lists_sem)
+    fetch.start()
+    places = []
+    for group in range(GROUPS):
+        for a in range(NB):
+            lane = inverse_ref[pl.ds(group * 128 + a, 8, stride=16), :].astype(jnp.int32)
+            block = inverse_ref[pl.ds(group * 128 + 8 + a, 8, stride=16), :].astype(jnp.int32)
+            places.append((lane, block))
+    fetch.wait()
     for d in range(SLOTS):
-        block = send_ref[0, d]
+        block = lists_ref[3, d]
         grain = block >> 2
         row = ((grain >> 3) * SB + (block & 3)) * 24 + (grain & 7)
         block_ref[pl.ds(row, 3, stride=8), :] = back_ref[3 * d : 3 * d + 3, :]
+    done = []
     for group in range(GROUPS):
         grains = pl.ds(8 * group, 8)
-        bond_ref = bond_refs[group * bonds // GROUPS]
-        bond_grains = pl.ds((8 * group) % (GRAINS_DEV // bonds), 8)
+        part = max(n for n in range(bonds) if BOND_PARTS[n][0] <= 8 * group)
+        bond_ref = bond_refs[part]
+        bond_grains = pl.ds(8 * group - BOND_PARTS[part][0], 8)
         for a in range(NB):
-            lane = inverse_ref[pl.ds(group * 128 + a, 8, stride=16), :].astype(jnp.int32)
-            block = inverse_ref[pl.ds(group * 128 + 8 + a, 8, stride=16), :].astype(jnp.int32)
+            lane, block = places[group * NB + a]
             columns = slice(a * BLK, (a + 1) * BLK)
             for c in range(3):
                 value = jnp.zeros((8, BLK), F32)
@@ -473,20 +576,33 @@
                 force = bond_ref[c, bond_grains, columns] + value
                 force_ref[c, grains, columns] = force
                 new_ref[c, grains, columns] = vel_ref[c, grains, columns] + TIME_STEP * force
-
-
-def sum_forces(send_order, returned, inverse, velocity, bonds):
+        for n, (source, target) in enumerate(((force_ref, force_hbm), (new_ref, new_hbm))):
+            done.append(pltpu.make_async_copy(source.at[:, grains], target.at[:, grains], out_sems.at[group, n]))
+            done[-1].start()
+    for copy in done:
+        copy.wait()
+
+
+def sum_forces(lists, returned, inverse, velocity, bonds):
     vmem = pl.BlockSpec(memory_space=pltpu.VMEM)
-    shape = jax.ShapeDtypeStruct((3, GRAINS_DEV, NODES), F32)
+    hbm = pl.BlockSpec(memory_space=pltpu.HBM)
+    shape = (3, GRAINS_DEV, NODES)
     return pl.pallas_call(
         functools.partial(sum_kernel, len(bonds)),
-        out_shape=(shape, shape),
-        in_specs=[pl.BlockSpec(memory_space=pltpu.SMEM)] + [vmem] * (3 + len(bonds)),
-        out_specs=(vmem, vmem),
-        scratch_shapes=[pltpu.VMEM((SLOTS * 3, BLK), F32)],
+        out_shape=(jax.ShapeDtypeStruct(shape, F32),) * 2,
+        in_specs=[pl.BlockSpec(memory_space=pl.ANY)] + [vmem] * (3 + len(bonds)),
+        out_specs=(hbm, hbm),
+        scratch_shapes=[
+            pltpu.SMEM((8, SLOTS), jnp.int32),
+            pltpu.VMEM(shape, F32),
+            pltpu.VMEM(shape, F32),
+            pltpu.VMEM((SLOTS * 3, BLK), F32),
+            pltpu.SemaphoreType.DMA,
+            pltpu.SemaphoreType.DMA((GROUPS, 2)),
+        ],
         compiler_params=pltpu.CompilerParams(vmem_limit_bytes=8 * MIB),
         name="sum_forces",
-    )(send_order, returned, inverse, velocity, *bonds)
+    )(lists, returned, inverse, velocity, *bonds)
 
 
 def exchange(rows, width):
@@ -510,17 +626,15 @@
     displacement = displacement.transpose(1, 0, 2)
     velocity = velocity.transpose(1, 0, 2)
     tiles = tile_list.transpose(1, 2, 0)
-    pairs = pair_list[0].T
     words = broken_bits.reshape(GRAINS_DEV, TILES, 16, BLK).transpose(0, 2, 1, 3).reshape(GRAINS_DEV * 64, BLK)
     outgoing = surface_blocks(send_order, displacement, velocity, centers, surface_nodes)
     received = exchange(outgoing, 6)
-    half = GRAINS_DEV // 2
-    bonds = [bond_forces(first, half, tiles, displacement, words) for first in (0, half)]
-    inverse = surface_places(surface_nodes)
-    received, bonds[0] = lax.optimization_barrier((received, bonds[0]))
-    slot_force = contact_forces(pair_count, pairs, received)
+    inverse, lists = surface_places(pair_count, surface_nodes, pair_list[0].T, send_order)
+    bonds = [bond_forces(first, count, tiles, displacement, words) for first, count in BOND_PARTS]
+    received, lists, bonds[0] = lax.optimization_barrier((received, lists, bonds[0]))
+    slot_force = contact_forces(lists, received)
     returned = exchange(slot_force, 3)
-    force, new_velocity = sum_forces(send_order, returned, inverse, velocity, bonds)
+    force, new_velocity = sum_forces(lists, returned, inverse, velocity, bonds)
     return force.transpose(1, 0, 2), new_velocity.transpose(1, 0, 2)
 
 

time: 56.4 us -> 51 us (0.904)
  starting transfers between devices: 19 us -> 15.1 us
  local copies, waits for them, and re-layouts: 4.13 us -> 0.65 us
  Pallas kernels: 18.8 us -> 21 us
    all_to_all x2, starting transfers between devices: 19 us -> 15.1 us  [exchange(): lax.all_to_all(rows.reshape(SLOTS, 1, width, BLK), ('grain', 'cell'), spl...]
    unnamed x22 -> x14, local copies, waits for them, and re-layouts: 4.13 us -> 0.65 us
    pallas_call x1, Pallas kernels: 4.23 us -> 6.19 us  [contact_forces(): pl.pallas_call(contact_kernel, out_shape=jax.ShapeDtypeStruct((SLOTS * 3,...]
    pallas_call x1, Pallas kernels: 2.44 us -> 3.23 us  [surface_blocks(): pl.pallas_call(gather_kernel, out_shape=jax.ShapeDtypeStruct((SLOTS * 6,...]
where the time goes in v1:
time: 51 us; the launch traced here: 50.8 us
  Pallas kernels  21 us (41%)
  starting transfers between devices  15.1 us (30%)
  waiting for transfers between devices  12.7 us (25%)
  between operations  1.4 us (3%)
  local copies, waits for them, and re-layouts  0.65 us (1%)
    all_to_all x2, starting transfers between devices, exchange(): lax.all_to_all(rows.reshape(SLOTS, 1, width, BLK), ('grain', 'cell'), spl...  15.1 us
    all_to_all x2, waiting for transfers between devices, exchange(): lax.all_to_all(rows.reshape(SLOTS, 1, width, BLK), ('grain', 'cell'), spl...  12.7 us
    pallas_call x2, Pallas kernels, bond_forces(): pl.pallas_call(functools.partial(bond_kernel, first_grain, grains), out_s...  7.83 us
    pallas_call x1, Pallas kernels, contact_forces(): pl.pallas_call(contact_kernel, out_shape=jax.ShapeDtypeStruct((SLOTS * 3,...  6.19 us
    pallas_call x1, Pallas kernels, surface_blocks(): pl.pallas_call(gather_kernel, out_shape=jax.ShapeDtypeStruct((SLOTS * 6,...  3.23 us
    pallas_call x1, Pallas kernels, sum_forces(): pl.pallas_call(functools.partial(sum_kernel, len(bonds)), out_shape=(jax....  2.18 us
    pallas_call x1, Pallas kernels, surface_places(): pl.pallas_call(inverse_kernel, out_shape=(jax.ShapeDtypeStruct((GRAINS_DE...  1.56 us
  transfers between devices with their start and end apart: 2, of which 2 were waited for; matrix products, arithmetic and copies ran while one was open for 0% of the time, Pallas kernels for 18%

profile of v1, /device:TPU:1, one launch (start us, length us, event | category | flops | bytes accessed | tf_op | source)
XLA Modules:
  0.0 50.8 jit_solution(6797370187524703598)
XLA Ops:
  0.6 3.2 %surface_blocks.1 = f32[768,128]{1,0:T(8,128)} custom-call(s32[1,128]{1,0:T(1,128)} %send_ref.1, f32[3,32,768]{2,1,0:T(8,128)} %bitcast.21, f32[3,32,768]{2,1,0:T(8,128)} %bitcast.18, f32[3,32]{1,0:T(4,128)} %centers_hbm.1, s32[32,512]{1,0:T(8,128)} %nodes_ref.1), custom_call_target="tpu_custom_call" | custom-call | tf_op jit(solution)/shard_map/surface_blocks/pallas_call | solution.py:146
  3.9 0.0 copy-start.2
  3.9 0.0 copy-start.6
  3.9 11.5 %all-to-all-start = ((f32[128,1,6,128]{3,1,2,0:T(1,128)}), f32[128,1,6,128]{3,1,2,0:T(1,128)S(1)}, u32[]{:S(2)}, u32[]{:S(2)}) async-start(f32[128,1,6,128]{3,1,2,0:T(1,128)} %bitcast.29), calls=%async_computation | async-start | bytes 786432 | tf_op jit(solution)/shard_map/all_to_all | solution.py:609
  16.0 0.0 copy-start.3
  16.0 0.0 copy-start.4
  16.1 0.0 copy-done.2
  16.1 0.0 copy-done.6
  16.1 0.6 %copy-done.3 = s32[1,128]{1,0:T(1,128)S(1)} copy-done((s32[1,128]{1,0:T(1,128)S(1)}, s32[1,128]{1,0:T(1,128)}, u32[]{:S(2)}) %copy-start.3) | copy-done | bytes 536
  16.7 0.0 copy-start.1
  16.7 0.0 copy-start.5
  16.7 1.6 %surface_places.1 = (f32[512,128]{1,0:T(8,128)S(1)}, s32[8,128]{1,0:T(8,128)S(1)}) custom-call(s32[1]{0:T(128)S(6)} %copy.16.count_ref, s32[32,512]{1,0:T(8,128)S(1)} %copy-done.2, s32[2,128]{1,0:T(2,128)S(1)} %bitcast.28, s32[1,128]{1,0:T(1,128)S(1)} %copy-done.3), custom_call_target="tpu_custom_call" | custom-call | flops 500000000 | bytes 500000 | tf_op jit(solution)/shard_map/surface_places/pallas_call | solution.py:531
  18.3 0.0 copy-done.4
  18.3 0.0 copy-done.1
  18.3 0.0 copy-done.5
  18.3 2.8 %bond_forces.2.refs_0_ = f32[3,8,768]{2,1,0:T(8,128)S(1)} custom-call(s32[4,2,32]{2,1,0:T(2,128)S(1)} %bitcast.26, f32[3,32,768]{2,1,0:T(8,128)S(1)} %bitcast.22, s32[2048,128]{1,0:T(8,128)S(1)} %bitcast.24), custom_call_target="tpu_custom_call" | custom-call | flops 2000000000 | bytes 2000000 | tf_op jit(solution)/shard_map/bond_forces/pallas_call | solution.py:482
  21.1 7.0 %all-to-all-done = f32[128,1,6,128]{3,1,2,0:T(1,128)S(1)} async-done(((f32[128,1,6,128]{3,1,2,0:T(1,128)}), f32[128,1,6,128]{3,1,2,0:T(1,128)S(1)}, u32[]{:S(2)}, u32[]{:S(2)}) %all-to-all-start) | async-done | bytes 393248 | tf_op jit(solution)/shard_map/all_to_all | solution.py:609
  28.1 6.2 %contact_forces.1 = f32[384,128]{1,0:T(8,128)} custom-call(s32[8,128]{1,0:T(8,128)S(1)} %get-tuple-element.10.lists_hbm, f32[768,128]{1,0:T(8,128)S(1)} %bitcast.17), custom_call_target="tpu_custom_call" | custom-call | tf_op jit(solution)/shard_map/contact_forces/pallas_call | solution.py:292
  34.3 3.6 %all-to-all-start.1 = ((f32[128,1,3,128]{3,1,2,0:T(1,128)}), f32[128,1,3,128]{3,1,2,0:T(1,128)S(1)}, u32[]{:S(2)}, u32[]{:S(2)}) async-start(f32[128,1,3,128]{3,1,2,0:T(1,128)} %bitcast.10), calls=%async_computation.1 | async-start | bytes 393216 | tf_op jit(solution)/shard_map/all_to_all | solution.py:609
  37.9 0.0 copy-start
  37.9 5.0 %bond_forces.3.refs_1_ = f32[3,24,768]{2,1,0:T(8,128)S(1)} custom-call(s32[4,2,32]{2,1,0:T(2,128)S(1)} %bitcast.27, f32[3,32,768]{2,1,0:T(8,128)S(1)} %bitcast.23, s32[2048,128]{1,0:T(8,128)S(1)} %bitcast.25), custom_call_target="tpu_custom_call" | custom-call | flops 2000000000 | bytes 2000000 | tf_op jit(solution)/shard_map/bond_forces/pallas_call | solution.py:482
  43.0 5.7 %all-to-all-done.1 = f32[128,1,3,128]{3,1,2,0:T(1,128)S(1)} async-done(((f32[128,1,3,128]{3,1,2,0:T(1,128)}), f32[128,1,3,128]{3,1,2,0:T(1,128)S(1)}, u32[]{:S(2)}, u32[]{:S(2)}) %all-to-all-start.1) | async-done | bytes 196640 | tf_op jit(solution)/shard_map/all_to_all | solution.py:609
  48.6 0.0 copy-done
  48.6 2.2 %sum_forces.1 = (f32[3,32,768]{2,1,0:T(8,128)}, f32[3,32,768]{2,1,0:T(8,128)}) custom-call(s32[8,128]{1,0:T(8,128)S(1)} %get-tuple-element.10.lists_hbm, f32[384,128]{1,0:T(8,128)S(1)} %bitcast.20, f32[512,128]{1,0:T(8,128)S(1)} %get-tuple-element.12.inverse_ref, f32[3,32,768]{2,1,0:T(8,128)S(1)} %bitcast.19, f32[3,8,768]{2,1,0:T(8,128)S(1)} %bond_forces.2.refs_0_, ...), custom_call_target="tpu_custom_call" | custom-call | tf_op jit(solution)/shard_map/sum_forces/pallas_call | solution.py:590
Async XLA Ops:
  3.9 12.2 %copy-start.2 = (s32[32,512]{1,0:T(8,128)S(1)}, s32[32,512]{1,0:T(8,128)}, u32[]{:S(2)}) copy-start(s32[32,512]{1,0:T(8,128)} %nodes_ref.1) | copy-start | bytes 196612
  3.9 12.2 %copy-start.6 = (s32[1,128,2]{1,2,0:T(2,128)S(1)}, s32[1,128,2]{1,2,0:T(2,128)}, u32[]{:S(2)}) copy-start(s32[1,128,2]{1,2,0:T(2,128)} %param.16) | copy-start | bytes 3076
  3.9 24.2 %all-to-all-start = ((f32[128,1,6,128]{3,1,2,0:T(1,128)}), f32[128,1,6,128]{3,1,2,0:T(1,128)S(1)}, u32[]{:S(2)}, u32[]{:S(2)}) async-start(f32[128,1,6,128]{3,1,2,0:T(1,128)} %bitcast.29), calls=%async_computation | async-start | bytes 786432 | tf_op jit(solution)/shard_map/all_to_all | solution.py:609
  16.0 0.7 %copy-start.3 = (s32[1,128]{1,0:T(1,128)S(1)}, s32[1,128]{1,0:T(1,128)}, u32[]{:S(2)}) copy-start(s32[1,128]{1,0:T(1,128)} %send_ref.1) | copy-start | bytes 1540
  16.0 2.2 %copy-start.4 = (s32[32,4,2048]{2,1,0:T(4,128)S(1)}, s32[32,4,2048]{2,1,0:T(4,128)}, u32[]{:S(2)}) copy-start(s32[32,4,2048]{2,1,0:T(4,128)} %param.13) | copy-start | bytes 3145732
  16.7 1.6 %copy-start.1 = (f32[32,3,768]{2,0,1:T(8,128)S(1)}, f32[32,3,768]{2,0,1:T(8,128)}, u32[]{:S(2)}) copy-start(f32[32,3,768]{2,0,1:T(8,128)} %param.9) | copy-start | bytes 884740
  16.7 1.6 %copy-start.5 = (s32[32,4,2]{0,2,1:T(2,128)S(1)}, s32[32,4,2]{0,2,1:T(2,128)}, u32[]{:S(2)}) copy-start(s32[32,4,2]{0,2,1:T(2,128)} %param.12) | copy-start | bytes 3076
  34.3 14.3 %all-to-all-start.1 = ((f32[128,1,3,128]{3,1,2,0:T(1,128)}), f32[128,1,3,128]{3,1,2,0:T(1,128)S(1)}, u32[]{:S(2)}, u32[]{:S(2)}) async-start(f32[128,1,3,128]{3,1,2,0:T(1,128)} %bitcast.10), calls=%async_computation.1 | async-start | bytes 393216 | tf_op jit(solution)/shard_map/all_to_all | solution.py:609
  37.9 10.7 %copy-start = (f32[32,3,768]{2,0,1:T(8,128)S(1)}, f32[32,3,768]{2,0,1:T(8,128)}, u32[]{:S(2)}) copy-start(f32[32,3,768]{2,0,1:T(8,128)} %param.10) | copy-start | bytes 884740

commit v2 on v1

--- a/solution.py
+++ b/solution.py
@@ -110,8 +110,9 @@
             )
             for c in range(3)
         ]
-        for copy in large[group]:
-            copy.wait()
+        if group % 2 == 0:
+            for copy in large[group] + large[group + 1]:
+                copy.wait()
         for k in range(SB):
             node = nodes_ref[grains, k * BLK : (k + 1) * BLK]
             lane = node & (BLK - 1)
@@ -125,14 +126,12 @@
                     value = jnp.where(block == a, lane_gather(source, lane), value)
                 if c < 3:
                     value = rest[c].astype(F32) + value + offsets[c]
-                state_ref[pl.ds((group * SB + k) * 48 + c * 8, 8), :] = value
+                state_ref[pl.ds(group * 256 + k * 8 + c, 8, stride=32), :] = value
     small[1].wait()
     done = []
     for d in range(SLOTS):
-        block = send_ref[0, d]
-        grain = block >> 2
-        row = ((grain >> 3) * SB + (block & 3)) * 48 + (grain & 7)
-        out_ref[6 * d : 6 * d + 6, :] = state_ref[pl.ds(row, 6, stride=8), :]
+        row = pl.multiple_of(send_ref[0, d] * 8, 8)
+        out_ref[6 * d : 6 * d + 6, :] = state_ref[pl.ds(row, 8), :][:6]
         if d % 32 == 31:
             part = pl.ds(6 * (d - 31), 192)
             done.append(pltpu.make_async_copy(out_ref.at[part], out_hbm.at[part], out_sems.at[d // 32]))
@@ -154,7 +153,7 @@
             pltpu.VMEM((3, GRAINS_DEV, NODES), F32),
             pltpu.VMEM((3, GRAINS_DEV), F32),
             pltpu.VMEM((GRAINS_DEV, SB * BLK), jnp.int32),
-            pltpu.VMEM((SLOTS * 6, BLK), F32),
+            pltpu.VMEM((SLOTS * 8, BLK), F32),
             pltpu.VMEM((SLOTS * 6, BLK), F32),
             pltpu.SemaphoreType.DMA((2,)),
             pltpu.SemaphoreType.DMA((GROUPS, 3)),
@@ -165,7 +164,7 @@
     )(send_order, displacement, velocity, centers, surface_nodes)
 
 
-PAIR_UNROLL = 32
+PAIR_UNROLL = 64
 
 
 def contact_kernel(
@@ -213,7 +212,7 @@
         put(slide_ref, 16, group, slide)
         return carry
 
-    lax.fori_loop(0, SLOTS // 8, prepare, 0, unroll=4)
+    lax.fori_loop(0, SLOTS // 8, prepare, 0, unroll=8)
     acc_ref[...] = jnp.zeros_like(acc_ref)
     fetch.wait()
     total = lists_ref[2, 0]
@@ -221,10 +220,10 @@
     def rows(ref, count, slot):
         return ref[pl.ds((slot >> 3) * (count * 8) + (slot & 7), count, stride=8), :]
 
-    def batch(step, carry):
+    def batch(first, pairs):
         chosen = []
-        for n in range(PAIR_UNROLL):
-            flat = step * PAIR_UNROLL + n
+        for n in range(pairs):
+            flat = first + n
             in_range = flat < total
             at = jnp.minimum(flat, SLOTS - 1)
             i = jnp.where(in_range, lists_ref[0, at], 0)
@@ -258,9 +257,18 @@
             acc_ref[rows_i, :] += to_i
             rows_j = pl.ds(pl.multiple_of(j * 16, 16), 16)
             acc_ref[rows_j, :] += to_j
+
+    def full_batch(step, carry):
+        batch(step * PAIR_UNROLL, PAIR_UNROLL)
         return carry
 
-    lax.fori_loop(0, (total + PAIR_UNROLL - 1) // PAIR_UNROLL, batch, 0)
+    half = PAIR_UNROLL // 2
+    whole = (total + half - 1) // PAIR_UNROLL
+    lax.fori_loop(0, whole, full_batch, 0)
+
+    @pl.when(total > whole * PAIR_UNROLL)
+    def _():
+        batch(whole * PAIR_UNROLL, half)
 
     def finish(group):
         def acc(n):
@@ -504,7 +512,9 @@
 def inverse_kernel(count_ref, nodes_ref, pairs_ref, send_ref, out_ref, lists_ref):
     lists_ref[:2, :] = pairs_ref[...]
     lists_ref[2:3, :] = jnp.full((1, SLOTS), count_ref[0], jnp.int32)
-    lists_ref[3:4, :] = send_ref[...]
+    block = send_ref[...]
+    grain = block >> 2
+    lists_ref[3:4, :] = ((grain >> 3) * SB + (block & 3)) * 24 + (grain & 7)
     lists_ref[4:, :] = jnp.zeros((4, SLOTS), jnp.int32)
     sub128 = sublane_iota((BLK, SB * BLK))
     sub16 = sublane_iota((16, SB * BLK))
@@ -555,10 +565,7 @@
             places.append((lane, block))
     fetch.wait()
     for d in range(SLOTS):
-        block = lists_ref[3, d]
-        grain = block >> 2
-        row = ((grain >> 3) * SB + (block & 3)) * 24 + (grain & 7)
-        block_ref[pl.ds(row, 3, stride=8), :] = back_ref[3 * d : 3 * d + 3, :]
+        block_ref[pl.ds(lists_ref[3, d], 3, stride=8), :] = back_ref[3 * d : 3 * d + 3, :]
     done = []
     for group in range(GROUPS):
         grains = pl.ds(8 * group, 8)

time: 51 us -> 50 us (0.980)
  Pallas kernels: 21 us -> 17.8 us
  starting transfers between devices: 15.1 us -> 17.2 us
    pallas_call x1, Pallas kernels: 6.19 us -> 3.66 us  [contact_forces(): pl.pallas_call(contact_kernel, out_shape=jax.ShapeDtypeStruct((SLOTS * 3,...]
    all_to_all x2, starting transfers between devices: 15.1 us -> 17.2 us  [exchange(): lax.all_to_all(rows.reshape(SLOTS, 1, width, BLK), ('grain', 'cell'), spl...]
  transfers between devices with their start and end apart: 2 -> 2, of which waited for: 2 -> 2; matrix products, arithmetic and copies ran while one was open for 0% -> 0% of each run, Pallas kernels for 18% -> 19%
where the time goes in v2:
time: 50 us; the launch traced here: 49.7 us
  Pallas kernels  17.8 us (36%)
  starting transfers between devices  17.2 us (34%)
  waiting for transfers between devices  12.7 us (25%)
  between operations  1.4 us (3%)
  local copies, waits for them, and re-layouts  0.65 us (1%)
    all_to_all x2, starting transfers between devices, exchange(): lax.all_to_all(rows.reshape(SLOTS, 1, width, BLK), ('grain', 'cell'), spl...  17.2 us
    all_to_all x2, waiting for transfers between devices, exchange(): lax.all_to_all(rows.reshape(SLOTS, 1, width, BLK), ('grain', 'cell'), spl...  12.7 us
    pallas_call x2, Pallas kernels, bond_forces(): pl.pallas_call(functools.partial(bond_kernel, first_grain, grains), out_s...  7.85 us
    pallas_call x1, Pallas kernels, contact_forces(): pl.pallas_call(contact_kernel, out_shape=jax.ShapeDtypeStruct((SLOTS * 3,...  3.66 us
    pallas_call x1, Pallas kernels, surface_blocks(): pl.pallas_call(gather_kernel, out_shape=jax.ShapeDtypeStruct((SLOTS * 6,...  2.88 us
    pallas_call x1, Pallas kernels, sum_forces(): pl.pallas_call(functools.partial(sum_kernel, len(bonds)), out_shape=(jax....  1.87 us
    pallas_call x1, Pallas kernels, surface_places(): pl.pallas_call(inverse_kernel, out_shape=(jax.ShapeDtypeStruct((GRAINS_DE...  1.56 us
  transfers between devices with their start and end apart: 2, of which 2 were waited for; matrix products, arithmetic and copies ran while one was open for 0% of the time, Pallas kernels for 19%

profile of v2, /device:TPU:1, one launch (start us, length us, event | category | flops | bytes accessed | tf_op | source)
XLA Modules:
  0.0 49.7 jit_solution(1453618918503979615)
XLA Ops:
  0.6 2.9 %surface_blocks.1 = f32[768,128]{1,0:T(8,128)} custom-call(s32[1,128]{1,0:T(1,128)} %send_ref.1, f32[3,32,768]{2,1,0:T(8,128)} %bitcast.21, f32[3,32,768]{2,1,0:T(8,128)} %bitcast.18, f32[3,32]{1,0:T(4,128)} %centers_hbm.1, s32[32,512]{1,0:T(8,128)} %nodes_ref.1), custom_call_target="tpu_custom_call" | custom-call | tf_op jit(solution)/shard_map/surface_blocks/pallas_call | solution.py:145
  3.5 0.0 copy-start.2
  3.5 0.0 copy-start.6
  3.5 11.5 %all-to-all-start = ((f32[128,1,6,128]{3,1,2,0:T(1,128)}), f32[128,1,6,128]{3,1,2,0:T(1,128)S(1)}, u32[]{:S(2)}, u32[]{:S(2)}) async-start(f32[128,1,6,128]{3,1,2,0:T(1,128)} %bitcast.29), calls=%async_computation | async-start | bytes 786432 | tf_op jit(solution)/shard_map/all_to_all | solution.py:616
  15.7 0.0 copy-start.3
  15.7 0.0 copy-start.4
  15.7 0.0 copy-done.2
  15.7 0.0 copy-done.6
  15.7 0.6 %copy-done.3 = s32[1,128]{1,0:T(1,128)S(1)} copy-done((s32[1,128]{1,0:T(1,128)S(1)}, s32[1,128]{1,0:T(1,128)}, u32[]{:S(2)}) %copy-start.3) | copy-done | bytes 536
  16.3 0.0 copy-start.1
  16.3 0.0 copy-start.5
  16.3 1.6 %surface_places.1 = (f32[512,128]{1,0:T(8,128)S(1)}, s32[8,128]{1,0:T(8,128)S(1)}) custom-call(s32[1]{0:T(128)S(6)} %copy.16.count_ref, s32[32,512]{1,0:T(8,128)S(1)} %copy-done.2, s32[2,128]{1,0:T(2,128)S(1)} %bitcast.28, s32[1,128]{1,0:T(1,128)S(1)} %copy-done.3), custom_call_target="tpu_custom_call" | custom-call | flops 500000000 | bytes 500000 | tf_op jit(solution)/shard_map/surface_places/pallas_call | solution.py:541
  17.9 0.0 copy-done.4
  17.9 0.0 copy-done.1
  17.9 0.0 copy-done.5
  17.9 2.8 %bond_forces.2.refs_0_ = f32[3,8,768]{2,1,0:T(8,128)S(1)} custom-call(s32[4,2,32]{2,1,0:T(2,128)S(1)} %bitcast.26, f32[3,32,768]{2,1,0:T(8,128)S(1)} %bitcast.22, s32[2048,128]{1,0:T(8,128)S(1)} %bitcast.24), custom_call_target="tpu_custom_call" | custom-call | flops 2000000000 | bytes 2000000 | tf_op jit(solution)/shard_map/bond_forces/pallas_call | solution.py:490
  20.8 7.0 %all-to-all-done = f32[128,1,6,128]{3,1,2,0:T(1,128)S(1)} async-done(((f32[128,1,6,128]{3,1,2,0:T(1,128)}), f32[128,1,6,128]{3,1,2,0:T(1,128)S(1)}, u32[]{:S(2)}, u32[]{:S(2)}) %all-to-all-start) | async-done | bytes 393248 | tf_op jit(solution)/shard_map/all_to_all | solution.py:616
  27.7 3.7 %contact_forces.1 = f32[384,128]{1,0:T(8,128)} custom-call(s32[8,128]{1,0:T(8,128)S(1)} %get-tuple-element.10.lists_hbm, f32[768,128]{1,0:T(8,128)S(1)} %bitcast.17), custom_call_target="tpu_custom_call" | custom-call | tf_op jit(solution)/shard_map/contact_forces/pallas_call | solution.py:300
  31.4 5.7 %all-to-all-start.1 = ((f32[128,1,3,128]{3,1,2,0:T(1,128)}), f32[128,1,3,128]{3,1,2,0:T(1,128)S(1)}, u32[]{:S(2)}, u32[]{:S(2)}) async-start(f32[128,1,3,128]{3,1,2,0:T(1,128)} %bitcast.10), calls=%async_computation.1 | async-start | bytes 393216 | tf_op jit(solution)/shard_map/all_to_all | solution.py:616
  37.1 0.0 copy-start
  37.1 5.0 %bond_forces.3.refs_1_ = f32[3,24,768]{2,1,0:T(8,128)S(1)} custom-call(s32[4,2,32]{2,1,0:T(2,128)S(1)} %bitcast.27, f32[3,32,768]{2,1,0:T(8,128)S(1)} %bitcast.23, s32[2048,128]{1,0:T(8,128)S(1)} %bitcast.25), custom_call_target="tpu_custom_call" | custom-call | flops 2000000000 | bytes 2000000 | tf_op jit(solution)/shard_map/bond_forces/pallas_call | solution.py:490
  42.2 5.7 %all-to-all-done.1 = f32[128,1,3,128]{3,1,2,0:T(1,128)S(1)} async-done(((f32[128,1,3,128]{3,1,2,0:T(1,128)}), f32[128,1,3,128]{3,1,2,0:T(1,128)S(1)}, u32[]{:S(2)}, u32[]{:S(2)}) %all-to-all-start.1) | async-done | bytes 196640 | tf_op jit(solution)/shard_map/all_to_all | solution.py:616
  47.8 0.0 copy-done
  47.8 1.9 %sum_forces.1 = (f32[3,32,768]{2,1,0:T(8,128)}, f32[3,32,768]{2,1,0:T(8,128)}) custom-call(s32[8,128]{1,0:T(8,128)S(1)} %get-tuple-element.10.lists_hbm, f32[384,128]{1,0:T(8,128)S(1)} %bitcast.20, f32[512,128]{1,0:T(8,128)S(1)} %get-tuple-element.12.inverse_ref, f32[3,32,768]{2,1,0:T(8,128)S(1)} %bitcast.19, f32[3,8,768]{2,1,0:T(8,128)S(1)} %bond_forces.2.refs_0_, ...), custom_call_target="tpu_custom_call" | custom-call | tf_op jit(solution)/shard_map/sum_forces/pallas_call | solution.py:597
Async XLA Ops:
  3.5 12.2 %copy-start.2 = (s32[32,512]{1,0:T(8,128)S(1)}, s32[32,512]{1,0:T(8,128)}, u32[]{:S(2)}) copy-start(s32[32,512]{1,0:T(8,128)} %nodes_ref.1) | copy-start | bytes 196612
  3.5 12.2 %copy-start.6 = (s32[1,128,2]{1,2,0:T(2,128)S(1)}, s32[1,128,2]{1,2,0:T(2,128)}, u32[]{:S(2)}) copy-start(s32[1,128,2]{1,2,0:T(2,128)} %param.16) | copy-start | bytes 3076
  3.5 24.2 %all-to-all-start = ((f32[128,1,6,128]{3,1,2,0:T(1,128)}), f32[128,1,6,128]{3,1,2,0:T(1,128)S(1)}, u32[]{:S(2)}, u32[]{:S(2)}) async-start(f32[128,1,6,128]{3,1,2,0:T(1,128)} %bitcast.29), calls=%async_computation | async-start | bytes 786432 | tf_op jit(solution)/shard_map/all_to_all | solution.py:616
  15.7 0.7 %copy-start.3 = (s32[1,128]{1,0:T(1,128)S(1)}, s32[1,128]{1,0:T(1,128)}, u32[]{:S(2)}) copy-start(s32[1,128]{1,0:T(1,128)} %send_ref.1) | copy-start | bytes 1540
  15.7 2.2 %copy-start.4 = (s32[32,4,2048]{2,1,0:T(4,128)S(1)}, s32[32,4,2048]{2,1,0:T(4,128)}, u32[]{:S(2)}) copy-start(s32[32,4,2048]{2,1,0:T(4,128)} %param.13) | copy-start | bytes 3145732
  16.3 1.6 %copy-start.1 = (f32[32,3,768]{2,0,1:T(8,128)S(1)}, f32[32,3,768]{2,0,1:T(8,128)}, u32[]{:S(2)}) copy-start(f32[32,3,768]{2,0,1:T(8,128)} %param.9) | copy-start | bytes 884740
  16.3 1.6 %copy-start.5 = (s32[32,4,2]{0,2,1:T(2,128)S(1)}, s32[32,4,2]{0,2,1:T(2,128)}, u32[]{:S(2)}) copy-start(s32[32,4,2]{0,2,1:T(2,128)} %param.12) | copy-start | bytes 3076
  31.4 16.4 %all-to-all-start.1 = ((f32[128,1,3,128]{3,1,2,0:T(1,128)}), f32[128,1,3,128]{3,1,2,0:T(1,128)S(1)}, u32[]{:S(2)}, u32[]{:S(2)}) async-start(f32[128,1,3,128]{3,1,2,0:T(1,128)} %bitcast.10), calls=%async_computation.1 | async-start | bytes 393216 | tf_op jit(solution)/shard_map/all_to_all | solution.py:616
  37.1 10.7 %copy-start = (f32[32,3,768]{2,0,1:T(8,128)S(1)}, f32[32,3,768]{2,0,1:T(8,128)}, u32[]{:S(2)}) copy-start(f32[32,3,768]{2,0,1:T(8,128)} %param.10) | copy-start | bytes 884740
